TPU v7x, 32 devices: a whole 2x2x4 slice. The times are simulated.
32 devices in a mesh: row: 2 (over core), col: 16 (over z, y, x).
Axes of the slice: x: 2, y: 2, z: 4, core: 2. Of those that a mesh axis runs over, the one named last changes fastest.
Arguments:
- mat_a: bfloat16 [5120, 24576], P('row', 'col'), may hold values from -6 to 6
- mat_b: bfloat16 [24576, 4096], P('row', 'col'), may hold values from -0.15625 to 0.15625
- mask_a: int32 [40, 192], P('row', 'col'), may hold values from 0 to 1, as said below
- mask_b: int32 [192, 32], P('row', 'col'), may hold values 0 or 1
Outputs:
- product: bfloat16 [5120, 4096], P('row', 'col')
Inputs may be any that keep to these rules, and one draw needn't show every extreme that they name: `mask_a`: in each tile of 20 x 12 entries, the block rows holding an occupied block come first and each holds at least one; in every draw some tile has all 20 block rows occupied.
All inputs are finite; a program needn't handle non-finite values. No bound on the sum of `mask_b` on one device may be relied on, other than what follows from the above.
Results may differ from a plain program's by a relative error of at most 0.0025.
Values may be sent and summed in bfloat16 or wider, within the bound.
A program may use at most 128 MiB of HBM per device.

v0:
```python
import jax
import jax.numpy as jnp
from jax import lax
from jax.sharding import PartitionSpec as P

BLK = 128


def from_behind(value, axis, steps):
    count = lax.axis_size(axis)
    pairs = [(source, (source + steps) % count) for source in range(count)]
    return lax.ppermute(value, axis, pairs)


def mask_blocks(matrix, occupied):
    rows, columns = occupied.shape
    blocked = matrix.reshape(rows, matrix.shape[0] // rows, columns, matrix.shape[1] // columns)
    scaling = occupied.astype(matrix.dtype)[:, None, :, None]
    return (blocked * scaling).reshape(matrix.shape)


def live_rows(occupied):
    return jnp.sum(jnp.any(occupied > 0, axis=1).astype(jnp.int32))


def add_rows(accum, matrix_rows, right_tile, row_first, row_last):
    block = BLK

    def one_row(row_index, summed):
        row_block = lax.dynamic_slice_in_dim(matrix_rows, row_index * block, block, 0)
        result = jnp.dot(row_block, right_tile, preferred_element_type=jnp.float32)
        current = lax.dynamic_slice_in_dim(summed, row_index * block, block, 0)
        return lax.dynamic_update_slice_in_dim(summed, current + result, row_index * block, 0)

    return lax.fori_loop(row_first, row_last, one_row, accum)


def body(mat_a, mat_b, mask_a, mask_b):
    inner_rows = mat_a.shape[1]
    inner_blocks = mask_a.shape[1]
    flags_a = mask_a.astype(jnp.bfloat16)
    flags_b = mask_b.astype(jnp.bfloat16)
    own_a = mask_blocks(mat_a, mask_a)
    own_b = mask_blocks(mat_b[:inner_rows], mask_b[:inner_blocks])
    row_place = lax.axis_index("row")
    slot_pick = jnp.where(row_place == 0, 1, 0).astype(jnp.int32)
    send_b = lax.dynamic_slice_in_dim(mat_b, slot_pick * inner_rows, inner_rows, 0)
    send_flags = lax.dynamic_slice_in_dim(flags_b, slot_pick * inner_blocks, inner_blocks, 0)
    live_here = live_rows(mask_a)
    accum = jnp.zeros((mat_a.shape[0], mat_b.shape[1]), jnp.float32)
    next_a, next_flags = from_behind((mat_a, flags_a), "col", -1)
    live_next = live_rows(next_flags)
    next_b, next_marks = from_behind((send_b, send_flags), "row", -1)
    accum = add_rows(accum, own_a, own_b, 0, live_here)
    accum = add_rows(
        accum, mask_blocks(next_a, next_flags), mask_blocks(next_b, next_marks), 0, live_next
    )
    return accum.astype(jnp.bfloat16)


def solution(mesh):
    return jax.shard_map(
        body,
        mesh=mesh,
        in_specs=(P("row", "col"), P("row", "col"), P("row", "col"), P("row", "col")),
        out_specs=P("row", "col"),
        check_vma=False,
    )
```

profile of v0, /device:TPU:14, one launch (start us, length us, event | category | flops | bytes accessed | tf_op | source)
XLA Modules:
  0.0 235.3 jit_solution(15307952966585490892)
XLA Ops:
  0.0 10.6 %copy.9 = bf16[2560,1536]{0,1:T(8,128)(2,1)} copy(bf16[2560,1536]{1,0:T(8,128)(2,1)} %param.8) | data formatting | bytes 15728640 | tf_op args[0]
  11.2 1.4 collective-permute-start
  13.3 2.5 %constant_dynamic-slice_fusion.1 = (bf16[1536,256]{1,0:T(8,128)(2,1)}, bf16[1536,256]{1,0:T(8,128)(2,1)S(1)}) fusion(bf16[12288,256]{1,0:T(8,128)(2,1)} %param.9, s32[]{:T(128)S(6)} %select_n.21, bf16[192,8,2,128]{3,2,1,0:T(2,128)(2,1)S(1)} %bitcast.28), kind=kLoop, calls=%fused_computation.17 | loop fusion | flops 1572864 | bytes 3932164 | tf_op jit(solution)/shard_map/dynamic_slice | solution.py:47
  19.6 3.8 %bitcast_multiply_fusion.1 = bf16[2560,1536]{0,1:T(8,128)(2,1)} fusion(bf16[2560,1536]{0,1:T(8,128)(2,1)S(1)} %copy-done, bf16[192,8,20,128]{3,2,1,0:T(8,128)(2,1)S(1)} %bitcast.27), kind=kLoop, calls=%fused_computation.9 | loop fusion | flops 3932160 | bytes 23592960 | tf_op jit(solution)/shard_map/mul | solution.py:19
  23.4 1.7 broadcast_in_dim.2
  25.1 6.0 %while.20 = (s32[]{:T(128)}, f32[2560,256]{1,0:T(8,128)}, s32[]{:T(128)}, bf16[2560,1536]{0,1:T(8,128)(2,1)}, bf16[1536,256]{1,0:T(8,128)(2,1)S(1)}, /*index=5*/s32[]{:T(128)}, s32[]{:T(128)}, s32[]{:T(128)}, s32[]{:T(128)}) while((s32[]{:T(128)}, f32[2560,256]{1,0:T(8,128)}, s32[]{:T(128)}, bf16[2560,1536]{0,1:T(8,128)(2,1)}, ...), condition=%wide.region_3.4_spmd, body=%wide.region_2.3_spmd.sunk | while | flops 100696072 | bytes 1442963 | solution.py:35
  25.7 2.0 fusion.16
  28.4 2.0 fusion.16
  31.2 152.6 %collective-permute-done = bf16[20,12]{0,1:T(8,128)(2,1)S(1)} collective-permute-done((bf16[20,12]{0,1:T(8,128)(2,1)S(1)}, bf16[20,12]{0,1:T(8,128)(2,1)S(1)}, u32[]{:S(2)}, u32[]{:S(2)}) %collective-permute-start) | collective-permute-done | bytes 512 | tf_op jit(solution)/shard_map/ppermute | solution.py:12
  186.4 7.3 %bitcast_multiply_fusion = bf16[2560,1536]{0,1:T(8,128)(2,1)} fusion(bf16[2560,1536]{0,1:T(8,128)(2,1)} %collective-permute-done.1, bf16[192,8,20,128]{3,2,1,0:T(8,128)(2,1)S(1)} %bitcast.26), kind=kLoop, calls=%fused_computation.8 | loop fusion | flops 3932160 | bytes 23592960 | tf_op jit(solution)/shard_map/mul | solution.py:19
  193.8 40.3 %while.21 = (s32[]{:T(128)}, f32[2560,256]{1,0:T(8,128)S(1)}, s32[]{:T(128)}, bf16[2560,1536]{0,1:T(8,128)(2,1)}, bf16[1536,256]{1,0:T(8,128)(2,1)S(1)}, /*index=5*/s32[]{:T(128)}, s32[]{:T(128)}, s32[]{:T(128)}, s32[]{:T(128)}) while((s32[]{:T(128)}, f32[2560,256]{1,0:T(8,128)S(1)}, s32[]{:T(128)}, bf16[2560,1536]{0,1:T(8,128)(2,1)}, ...), condition=%wide.region_7.8_spmd, body=%wide.region_6.7_spmd.sunk | while | flops 100696072 | bytes 1442963 | solution.py:35
  194.4 1.3 fusion.19
  196.4 1.3 fusion.19
  198.4 1.3 fusion.19
  202.4 1.3 fusion.19
  204.3 1.3 fusion.19
  206.3 1.3 fusion.19
  208.3 1.3 fusion.19
  214.3 1.3 fusion.19
  216.3 1.3 fusion.19
  218.2 1.3 fusion.19
  224.2 1.3 fusion.19
  226.2 1.3 fusion.19
  228.2 1.3 fusion.19
  (36 shorter events, 18.1 us)
Async XLA Ops:
  0.0 11.2 %copy-start.2 = (s32[20,12]{0,1:T(8,128)S(1)}, s32[20,12]{0,1:T(8,128)}, u32[]{:S(2)}) copy-start(s32[20,12]{0,1:T(8,128)} %param.10) | copy-start | bytes 2884
  0.0 12.6 %copy-start.3 = (s32[96,2]{0,1:T(2,128)S(1)}, s32[96,2]{0,1:T(2,128)}, u32[]{:S(2)}) copy-start(s32[96,2]{0,1:T(2,128)} %param.11) | copy-start | bytes 2308
  10.6 174.5 %collective-permute-start.1 = (bf16[2560,1536]{0,1:T(8,128)(2,1)}, bf16[2560,1536]{0,1:T(8,128)(2,1)}, u32[]{:S(2)}, u32[]{:S(2)}) collective-permute-start(bf16[2560,1536]{0,1:T(8,128)(2,1)} %copy.9), channel_id=1, source_target_pairs={{0,15},{1,0},{2,1},{3,2},{4,3},{5,4},{6,5},{7,6},{8,7},{9,8},{10,9... | collective-permute-start | bytes 23592968 | tf_op jit(solution)/shard_map/ppermute | solution.py:12
  11.2 172.6 %collective-permute-start = (bf16[20,12]{0,1:T(8,128)(2,1)S(1)}, bf16[20,12]{0,1:T(8,128)(2,1)S(1)}, u32[]{:S(2)}, u32[]{:S(2)}) collective-permute-start(bf16[20,12]{0,1:T(8,128)(2,1)S(1)} %convert_element_type.16), channel_id=1, source_target_pairs={{0,15},{1,0},{2,1},{3,2},{4,3},{5,4},{6,5},{7,6},{8,7},{9,8},{10,9... | collective-permute-start | bytes 1448 | tf_op jit(solution)/shard_map/ppermute | solution.py:12
  15.8 168.7 %collective-permute-start.2 = (bf16[1536,256]{1,0:T(8,128)(2,1)}, bf16[1536,256]{1,0:T(8,128)(2,1)S(1)}, u32[]{:S(2)}, u32[]{:S(2)}) collective-permute-start(bf16[1536,256]{1,0:T(8,128)(2,1)} %get-tuple-element.93), channel_id=1, source_target_pairs={{0,16},{16,0},{1,17},{17,1},{2,18},{18,2},{3,19},{19,3},{4,20},{20... | collective-permute-start | bytes 2359304 | tf_op jit(solution)/shard_map/ppermute | solution.py:12
  15.8 15.2 %collective-permute-start.3 = (bf16[12,2]{0,1:T(2,128)(2,1)S(1)}, bf16[12,2]{0,1:T(2,128)(2,1)S(1)}, u32[]{:S(2)}, u32[]{:S(2)}) collective-permute-start(bf16[12,2]{0,1:T(2,128)(2,1)S(1)} %get-tuple-element.95), channel_id=1, source_target_pairs={{0,16},{16,0},{1,17},{17,1},{2,18},{18,2},{3,19},{19,3},{4,20},{20... | collective-permute-start | bytes 152 | tf_op jit(solution)/shard_map/ppermute | solution.py:12
  16.3 3.2 %copy-start = (bf16[2560,1536]{0,1:T(8,128)(2,1)S(1)}, bf16[2560,1536]{0,1:T(8,128)(2,1)}, u32[]{:S(2)}) copy-start(bf16[2560,1536]{0,1:T(8,128)(2,1)} %copy.9) | copy-start | bytes 23592964
  186.4 7.3 %copy-start.1 = (f32[2560,256]{1,0:T(8,128)S(1)}, f32[2560,256]{1,0:T(8,128)}, u32[]{:S(2)}) copy-start(f32[2560,256]{1,0:T(8,128)} %get-tuple-element.189) | copy-start | bytes 7864324
where the time goes:
time: 239 us; the launch traced here: 235 us
  waiting for transfers between devices  153 us (64%)
  matrix products  30.5 us (13%)
  local copies, waits for them, and re-layouts  17.4 us (7%)
  other arithmetic  16.5 us (7%)
  loops' own time  15.8 us (7%)
  starting transfers between devices  2.48 us (1%)
    ppermute x4, waiting for transfers between devices, from_behind(): return lax.ppermute(value, axis, pairs)  153 us
    dot_general x22, matrix products, one_row(): result = jnp.dot(row_block, right_tile, preferred_element_type=jnp.float32)  30.5 us
    another operation x2, loops' own time, add_rows(): return lax.fori_loop(row_first, row_last, one_row, accum)  15.8 us
    unnamed x9, local copies, waits for them, and re-layouts  11.9 us
    mul x3, other arithmetic, mask_blocks(): return (blocked * scaling).reshape(matrix.shape)  11.3 us
  transfers between devices with their start and end apart: 4, of which 1 were waited for; matrix products, arithmetic and copies ran while one was open for 7% of the time, Pallas kernels for 0%

commit v1 on v0

v1 whole, which is shorter than its diff:
```python
import functools

import jax
import jax.numpy as jnp
from jax import lax
from jax.experimental import pallas as pl
from jax.experimental.pallas import tpu as pltpu
from jax.sharding import PartitionSpec as P

BLK = 128
LEVELS = 32767.0
TINY = 1e-33
MESH = pl.DeviceIdType.MESH


def times_flag(block, flag):
    scale = jnp.full(block.shape, flag.astype(jnp.float32)).astype(block.dtype)
    return block * scale


def kernel(
    group,
    a_hbm, b_hbm, flags_a, flags_b, out_ref,
    a_tile, b_own, b_raw, b_send, b_recv, own_sum, code_send, code_recv, step_send, step_recv,
    a_sem, b_sem, bs_sem, br_sem, cs_sem, cr_sem, ss_sem, sr_sem,
):
    n_row, n_col = lax.axis_size("row"), lax.axis_size("col")
    row, col = lax.axis_index("row"), lax.axis_index("col")
    up, down = lax.rem(row + n_row - 1, n_row), lax.rem(row + 1, n_row)
    left, right = lax.rem(col + n_col - 1, n_col), lax.rem(col + 1, n_col)
    rows, inner = a_tile.shape
    width = b_own.shape[1]
    deep, halves = inner // BLK, width // BLK
    span = group * BLK
    chunks = rows // span

    def piece(c):
        return pl.ds(pl.multiple_of(c * span, span), span)

    def load_a(c):
        return pltpu.make_async_copy(a_hbm.at[piece(c), :], a_tile.at[piece(c), :], a_sem.at[c])

    slot = jnp.where(row == 0, 1, 0)
    get_send = pltpu.make_async_copy(
        b_hbm.at[pl.ds(pl.multiple_of(slot * inner, inner), inner), :], b_raw, b_sem.at[0]
    )
    get_own = pltpu.make_async_copy(b_hbm.at[pl.ds(0, inner), :], b_own, b_sem.at[1])

    barrier = pltpu.get_barrier_semaphore()
    pl.semaphore_signal(barrier, inc=1, device_id={"row": down, "col": left}, device_id_type=MESH)
    pl.semaphore_signal(barrier, inc=1, device_id={"row": row, "col": right}, device_id_type=MESH)
    get_send.start()
    get_own.start()
    for c in range(chunks):
        load_a(c).start()

    get_send.wait()
    for h in range(halves):
        for k in range(deep):
            block = b_raw[k * BLK:(k + 1) * BLK, h * BLK:(h + 1) * BLK]
            b_send[h, k * BLK:(k + 1) * BLK, :] = times_flag(block, flags_b[slot * deep + k, h])

    def move_b(h):
        return pltpu.make_async_remote_copy(
            src_ref=b_send.at[h], dst_ref=b_recv.at[h], send_sem=bs_sem.at[h], recv_sem=br_sem.at[h],
            device_id={"row": up, "col": right}, device_id_type=MESH,
        )

    pl.semaphore_wait(barrier, 2)
    for h in range(halves):
        move_b(h).start()

    get_own.wait()
    for h in range(halves):
        for k in range(deep):
            spot = (slice(k * BLK, (k + 1) * BLK), slice(h * BLK, (h + 1) * BLK))
            b_own[spot] = times_flag(b_own[spot], flags_b[k, h])

    def own_part(c, carry):
        load_a(c).wait()
        for g in range(group):
            lines = pl.ds(pl.multiple_of(c * span + g * BLK, BLK), BLK)
            for k in range(deep):
                block = a_tile[lines, k * BLK:(k + 1) * BLK]
                a_tile[lines, k * BLK:(k + 1) * BLK] = times_flag(block, flags_a[c * group + g, k])
        own_sum[piece(c), :] = jnp.dot(a_tile[piece(c), :], b_own[...], preferred_element_type=jnp.float32)
        return carry

    lax.fori_loop(0, chunks, own_part, 0)

    def move_code(i):
        return pltpu.make_async_remote_copy(
            src_ref=code_send.at[i], dst_ref=code_recv.at[i], send_sem=cs_sem.at[i], recv_sem=cr_sem.at[i],
            device_id={"row": row, "col": left}, device_id_type=MESH,
        )

    def move_step(i):
        return pltpu.make_async_remote_copy(
            src_ref=step_send.at[i], dst_ref=step_recv.at[i], send_sem=ss_sem.at[i], recv_sem=sr_sem.at[i],
            device_id={"row": row, "col": left}, device_id_type=MESH,
        )

    for h in range(halves):
        move_b(h).wait_recv()

        def next_part(c, carry, h=h):
            i = h * chunks + c
            value = jnp.dot(a_tile[piece(c), :], b_recv[h], preferred_element_type=jnp.float32)
            most = jnp.maximum(jnp.max(jnp.abs(value), axis=0, keepdims=True), TINY)
            step_send[i] = jnp.broadcast_to(most * (1.0 / LEVELS), step_send.shape[1:])
            code_send[i] = jnp.round(value * (LEVELS / most)).astype(jnp.int32).astype(jnp.int16)
            move_step(i).start()
            move_code(i).start()
            return carry

        lax.fori_loop(0, chunks, next_part, 0)

    for h in range(halves):

        def finish(c, carry, h=h):
            i = h * chunks + c
            move_step(i).wait_recv()
            move_code(i).wait_recv()
            code = code_recv[i].astype(jnp.int32).astype(jnp.float32)
            total = own_sum[piece(c), h * BLK:(h + 1) * BLK] + code * step_recv[i, 0:1, :]
            out_ref[piece(c), h * BLK:(h + 1) * BLK] = total.astype(out_ref.dtype)
            return carry

        lax.fori_loop(0, chunks, finish, 0)

    for h in range(halves):
        move_b(h).wait_send()

    def sent(i, carry):
        move_step(i).wait_send()
        move_code(i).wait_send()
        return carry

    lax.fori_loop(0, halves * chunks, sent, 0)


def body(mat_a, mat_b, mask_a, mask_b):
    rows, inner = mat_a.shape
    width = mat_b.shape[1]
    block_rows = mask_a.shape[0]
    group = 2 if block_rows % 2 == 0 else 1
    span = group * BLK
    chunks = rows // span
    halves = width // BLK
    sends = halves * chunks
    dma = pltpu.SemaphoreType.DMA
    return pl.pallas_call(
        functools.partial(kernel, group),
        out_shape=jax.ShapeDtypeStruct((rows, width), jnp.bfloat16),
        in_specs=[
            pl.BlockSpec(memory_space=pl.ANY),
            pl.BlockSpec(memory_space=pl.ANY),
            pl.BlockSpec(memory_space=pltpu.SMEM),
            pl.BlockSpec(memory_space=pltpu.SMEM),
        ],
        out_specs=pl.BlockSpec(memory_space=pltpu.VMEM),
        scratch_shapes=[
            pltpu.VMEM((rows, inner), jnp.bfloat16),
            pltpu.VMEM((inner, width), jnp.bfloat16),
            pltpu.VMEM((inner, width), jnp.bfloat16),
            pltpu.VMEM((halves, inner, BLK), jnp.bfloat16),
            pltpu.VMEM((halves, inner, BLK), jnp.bfloat16),
            pltpu.VMEM((rows, width), jnp.float32),
            pltpu.VMEM((sends, span, BLK), jnp.int16),
            pltpu.VMEM((sends, span, BLK), jnp.int16),
            pltpu.VMEM((sends, 8, BLK), jnp.float32),
            pltpu.VMEM((sends, 8, BLK), jnp.float32),
            dma((chunks,)), dma((2,)), dma((halves,)), dma((halves,)),
            dma((sends,)), dma((sends,)), dma((sends,)), dma((sends,)),
        ],
        compiler_params=pltpu.CompilerParams(collective_id=0, has_side_effects=True),
        name="cannon",
    )(mat_a, mat_b, mask_a, mask_b)


def solution(mesh):
    return jax.shard_map(
        body,
        mesh=mesh,
        in_specs=(P("row", "col"), P("row", "col"), P("row", "col"), P("row", "col")),
        out_specs=P("row", "col"),
        check_vma=False,
    )
```

time: 239 us -> 80.9 us (0.34)
  the two profiles are of different devices: /device:TPU:14 before, /device:TPU:0 now
where the time goes in v1:
time: 80.9 us; the launch traced here: 80.6 us
  Pallas kernels  75.3 us (93%)
  local copies, waits for them, and re-layouts  5.23 us (6%)
    pallas_call x1, Pallas kernels, body(): pl.pallas_call(functools.partial(kernel, group), out_shape=jax.ShapeDtype...  75.3 us
    unnamed x3, local copies, waits for them, and re-layouts  5.23 us

profile of v1, /device:TPU:0, one launch (start us, length us, event | category | flops | bytes accessed | tf_op | source)
XLA Modules:
  0.0 80.6 jit_solution(2432778025940423929)
XLA Ops:
  0.0 1.4 %copy.5.flags_a = s32[20,12]{1,0:T(8,128)} copy(s32[20,12]{0,1:T(8,128)} %param.6) | data formatting | bytes 1920 | tf_op args[2]
  1.4 1.4 %copy.6.flags_b = s32[96,2]{1,0:T(8,128)} copy(s32[96,2]{0,1:T(2,128)} %param.7) | data formatting | bytes 1536 | tf_op args[3]
  2.8 75.3 %cannon.1 = bf16[2560,256]{1,0:T(8,128)(2,1)} custom-call(bf16[2560,1536]{1,0:T(8,128)(2,1)} %a_hbm.1, bf16[12288,256]{1,0:T(8,128)(2,1)} %b_hbm.1, s32[20,12]{1,0:T(8,128)} %copy.5.flags_a, s32[96,2]{1,0:T(8,128)} %copy.6.flags_b), custom_call_target="tpu_custom_call" | custom-call | tf_op jit(solution)/shard_map/cannon/pallas_call | solution.py:152
  78.1 2.5 %copy.8 = bf16[2560,256]{1,0:T(8,128)(2,1)} copy(bf16[2560,256]{1,0:T(8,128)(2,1)} %cannon.1) | data formatting | bytes 2621440

commit v2 on v1

--- a/solution.py
+++ b/solution.py
@@ -19,10 +19,10 @@
 
 
 def kernel(
-    group,
+    group, parts,
     a_hbm, b_hbm, flags_a, flags_b, out_ref,
-    a_tile, b_own, b_raw, b_send, b_recv, own_sum, code_send, code_recv, step_send, step_recv,
-    a_sem, b_sem, bs_sem, br_sem, cs_sem, cr_sem, ss_sem, sr_sem,
+    a_tile, b_own, b_raw, b_send, b_recv, b_pass, own_sum, code_send, code_recv, step_send, step_recv,
+    a_sem, b_sem, bs_sem, br_sem, ps_sem, pr_sem, cs_sem, cr_sem, ss_sem, sr_sem,
 ):
     n_row, n_col = lax.axis_size("row"), lax.axis_size("col")
     row, col = lax.axis_index("row"), lax.axis_index("col")
@@ -34,6 +34,12 @@
     span = group * BLK
     chunks = rows // span
 
+    relayed = n_col % 4 == 0
+    place = lax.rem(col, 4) if relayed else 0
+    ahead = lax.rem(col + 2, n_col)
+    behind = lax.rem(col + n_col - 2, n_col)
+    depth = inner // parts
+
     def piece(c):
         return pl.ds(pl.multiple_of(c * span, span), span)
 
@@ -47,7 +53,20 @@
     get_own = pltpu.make_async_copy(b_hbm.at[pl.ds(0, inner), :], b_own, b_sem.at[1])
 
     barrier = pltpu.get_barrier_semaphore()
-    pl.semaphore_signal(barrier, inc=1, device_id={"row": down, "col": left}, device_id_type=MESH)
+    if relayed:
+        @pl.when(place == 2)
+        def _():
+            pl.semaphore_signal(barrier, inc=1, device_id={"row": row, "col": right}, device_id_type=MESH)
+
+        @pl.when(place != 2)
+        def _():
+            pl.semaphore_signal(barrier, inc=1, device_id={"row": down, "col": left}, device_id_type=MESH)
+
+        @pl.when(place == 3)
+        def _():
+            pl.semaphore_signal(barrier, inc=1, device_id={"row": down, "col": behind}, device_id_type=MESH)
+    else:
+        pl.semaphore_signal(barrier, inc=1, device_id={"row": down, "col": left}, device_id_type=MESH)
     pl.semaphore_signal(barrier, inc=1, device_id={"row": row, "col": right}, device_id_type=MESH)
     get_send.start()
     get_own.start()
@@ -58,31 +77,70 @@
     for h in range(halves):
         for k in range(deep):
             block = b_raw[k * BLK:(k + 1) * BLK, h * BLK:(h + 1) * BLK]
-            b_send[h, k * BLK:(k + 1) * BLK, :] = times_flag(block, flags_b[slot * deep + k, h])
-
-    def move_b(h):
-        return pltpu.make_async_remote_copy(
-            src_ref=b_send.at[h], dst_ref=b_recv.at[h], send_sem=bs_sem.at[h], recv_sem=br_sem.at[h],
+            b_send[h, k * BLK:(k + 1) * BLK, :] = times_flag(block, flags_b[h, slot * deep + k])
+
+    def part(p):
+        return pl.ds(pl.multiple_of(p * depth, depth), depth)
+
+    def move_b(h, p):
+        return pltpu.make_async_remote_copy(
+            src_ref=b_send.at[h, part(p), :], dst_ref=b_recv.at[h, part(p), :],
+            send_sem=bs_sem.at[h, p], recv_sem=br_sem.at[h, p],
             device_id={"row": up, "col": right}, device_id_type=MESH,
         )
 
-    pl.semaphore_wait(barrier, 2)
-    for h in range(halves):
-        move_b(h).start()
+    def hand_over(h, p):
+        return pltpu.make_async_remote_copy(
+            src_ref=b_send.at[h, part(p), :], dst_ref=b_pass.at[h, part(p), :],
+            send_sem=bs_sem.at[h, p], recv_sem=pr_sem.at[h, p],
+            device_id={"row": up, "col": ahead}, device_id_type=MESH,
+        )
+
+    def pass_on(h, p):
+        return pltpu.make_async_remote_copy(
+            src_ref=b_pass.at[h, part(p), :], dst_ref=b_recv.at[h, part(p), :],
+            send_sem=ps_sem.at[h, p], recv_sem=br_sem.at[h, p],
+            device_id={"row": row, "col": left}, device_id_type=MESH,
+        )
+
+    pl.semaphore_wait(barrier, jnp.where(place == 3, 3, 2) if relayed else 2)
+    if relayed:
+        @pl.when(place == 1)
+        def _():
+            for h in range(halves):
+                for p in range(parts):
+                    hand_over(h, p).start()
+
+        @pl.when(place != 1)
+        def _():
+            for h in range(halves):
+                for p in range(parts):
+                    move_b(h, p).start()
+    else:
+        for h in range(halves):
+            for p in range(parts):
+                move_b(h, p).start()
 
     get_own.wait()
     for h in range(halves):
         for k in range(deep):
             spot = (slice(k * BLK, (k + 1) * BLK), slice(h * BLK, (h + 1) * BLK))
-            b_own[spot] = times_flag(b_own[spot], flags_b[k, h])
+            b_own[spot] = times_flag(b_own[spot], flags_b[h, k])
 
     def own_part(c, carry):
         load_a(c).wait()
+        if relayed:
+            @pl.when((place == 3) & (lax.rem(c, 2) == 0) & (c >= 2) & (c < 2 * parts + 2))
+            def _():
+                p = c // 2 - 1
+                hand_over(0, p).wait_recv()
+                pass_on(0, p).start()
+
         for g in range(group):
             lines = pl.ds(pl.multiple_of(c * span + g * BLK, BLK), BLK)
             for k in range(deep):
                 block = a_tile[lines, k * BLK:(k + 1) * BLK]
-                a_tile[lines, k * BLK:(k + 1) * BLK] = times_flag(block, flags_a[c * group + g, k])
+                a_tile[lines, k * BLK:(k + 1) * BLK] = times_flag(block, flags_a[k, c * group + g])
         own_sum[piece(c), :] = jnp.dot(a_tile[piece(c), :], b_own[...], preferred_element_type=jnp.float32)
         return carry
 
@@ -101,7 +159,15 @@
         )
 
     for h in range(halves):
-        move_b(h).wait_recv()
+        if relayed and h > 0:
+            @pl.when(place == 3)
+            def _(h=h):
+                for p in range(parts):
+                    hand_over(h, p).wait_recv()
+                    pass_on(h, p).start()
+
+        for p in range(parts):
+            move_b(h, p).wait_recv()
 
         def next_part(c, carry, h=h):
             i = h * chunks + c
@@ -129,7 +195,14 @@
         lax.fori_loop(0, chunks, finish, 0)
 
     for h in range(halves):
-        move_b(h).wait_send()
+        for p in range(parts):
+            move_b(h, p).wait_send()
+    if relayed:
+        @pl.when(place == 3)
+        def _():
+            for h in range(halves):
+                for p in range(parts):
+                    pass_on(h, p).wait_send()
 
     def sent(i, carry):
         move_step(i).wait_send()
@@ -148,9 +221,10 @@
     chunks = rows // span
     halves = width // BLK
     sends = halves * chunks
+    parts = 4 if mask_a.shape[1] % 4 == 0 and chunks >= 10 else 1
     dma = pltpu.SemaphoreType.DMA
     return pl.pallas_call(
-        functools.partial(kernel, group),
+        functools.partial(kernel, group, parts),
         out_shape=jax.ShapeDtypeStruct((rows, width), jnp.bfloat16),
         in_specs=[
             pl.BlockSpec(memory_space=pl.ANY),
@@ -165,17 +239,19 @@
             pltpu.VMEM((inner, width), jnp.bfloat16),
             pltpu.VMEM((halves, inner, BLK), jnp.bfloat16),
             pltpu.VMEM((halves, inner, BLK), jnp.bfloat16),
+            pltpu.VMEM((halves, inner, BLK), jnp.bfloat16),
             pltpu.VMEM((rows, width), jnp.float32),
             pltpu.VMEM((sends, span, BLK), jnp.int16),
             pltpu.VMEM((sends, span, BLK), jnp.int16),
             pltpu.VMEM((sends, 8, BLK), jnp.float32),
             pltpu.VMEM((sends, 8, BLK), jnp.float32),
-            dma((chunks,)), dma((2,)), dma((halves,)), dma((halves,)),
+            dma((chunks,)), dma((2,)), dma((halves, parts)), dma((halves, parts)),
+            dma((halves, parts)), dma((halves, parts)),
             dma((sends,)), dma((sends,)), dma((sends,)), dma((sends,)),
         ],
         compiler_params=pltpu.CompilerParams(collective_id=0, has_side_effects=True),
         name="cannon",
-    )(mat_a, mat_b, mask_a, mask_b)
+    )(mat_a, mat_b, mask_a.T, mask_b.T)
 
 
 def solution(mesh):

time: 80.9 us -> 80.8 us (level)
  the two profiles are of different devices: /device:TPU:0 before, /device:TPU:2 now
where the time goes in v2:
time: 80.8 us; the launch traced here: 80.6 us
  Pallas kernels  78.1 us (97%)
  local copies, waits for them, and re-layouts  2.46 us (3%)
    pallas_call x1, Pallas kernels, body(): pl.pallas_call(functools.partial(kernel, group, parts), out_shape=jax.Sha...  78.1 us
    unnamed x1, local copies, waits for them, and re-layouts  2.46 us

profile of v2, /device:TPU:2, one launch (start us, length us, event | category | flops | bytes accessed | tf_op | source)
XLA Modules:
  0.0 80.6 jit_solution(12627919039237597458)
XLA Ops:
  0.0 78.1 %cannon.1 = bf16[2560,256]{1,0:T(8,128)(2,1)} custom-call(bf16[2560,1536]{1,0:T(8,128)(2,1)} %a_hbm.1, bf16[12288,256]{1,0:T(8,128)(2,1)} %b_hbm.1, s32[12,20]{1,0:T(8,128)} %bitcast.2, s32[2,96]{1,0:T(2,128)} %bitcast.3), custom_call_target="tpu_custom_call" | custom-call | tf_op jit(solution)/shard_map/cannon/pallas_call | solution.py:226
  78.1 2.5 %copy.6 = bf16[2560,256]{1,0:T(8,128)(2,1)} copy(bf16[2560,256]{1,0:T(8,128)(2,1)} %cannon.1) | data formatting | bytes 2621440

commit v3 on v1

--- a/solution.py
+++ b/solution.py
@@ -58,7 +58,7 @@
     for h in range(halves):
         for k in range(deep):
             block = b_raw[k * BLK:(k + 1) * BLK, h * BLK:(h + 1) * BLK]
-            b_send[h, k * BLK:(k + 1) * BLK, :] = times_flag(block, flags_b[slot * deep + k, h])
+            b_send[h, k * BLK:(k + 1) * BLK, :] = times_flag(block, flags_b[h, slot * deep + k])
 
     def move_b(h):
         return pltpu.make_async_remote_copy(
@@ -74,7 +74,7 @@
     for h in range(halves):
         for k in range(deep):
             spot = (slice(k * BLK, (k + 1) * BLK), slice(h * BLK, (h + 1) * BLK))
-            b_own[spot] = times_flag(b_own[spot], flags_b[k, h])
+            b_own[spot] = times_flag(b_own[spot], flags_b[h, k])
 
     def own_part(c, carry):
         load_a(c).wait()
@@ -82,7 +82,7 @@
             lines = pl.ds(pl.multiple_of(c * span + g * BLK, BLK), BLK)
             for k in range(deep):
                 block = a_tile[lines, k * BLK:(k + 1) * BLK]
-                a_tile[lines, k * BLK:(k + 1) * BLK] = times_flag(block, flags_a[c * group + g, k])
+                a_tile[lines, k * BLK:(k + 1) * BLK] = times_flag(block, flags_a[k, c * group + g])
         own_sum[piece(c), :] = jnp.dot(a_tile[piece(c), :], b_own[...], preferred_element_type=jnp.float32)
         return carry
 
@@ -100,20 +100,24 @@
             device_id={"row": row, "col": left}, device_id_type=MESH,
         )
 
+    def send_out(i, carry):
+        move_step(i).start()
+        move_code(i).start()
+        return carry
+
+    def next_part(h, early, c, carry):
+        i = h * chunks + c
+        value = jnp.dot(a_tile[piece(c), :], b_recv[h], preferred_element_type=jnp.float32)
+        most = jnp.maximum(jnp.max(jnp.abs(value), axis=0, keepdims=True), TINY)
+        step_send[i] = jnp.broadcast_to(most * (1.0 / LEVELS), step_send.shape[1:])
+        code_send[i] = jnp.round(value * (LEVELS / most)).astype(jnp.int32).astype(jnp.int16)
+        return carry if early else send_out(i, carry)
+
     for h in range(halves):
         move_b(h).wait_recv()
-
-        def next_part(c, carry, h=h):
-            i = h * chunks + c
-            value = jnp.dot(a_tile[piece(c), :], b_recv[h], preferred_element_type=jnp.float32)
-            most = jnp.maximum(jnp.max(jnp.abs(value), axis=0, keepdims=True), TINY)
-            step_send[i] = jnp.broadcast_to(most * (1.0 / LEVELS), step_send.shape[1:])
-            code_send[i] = jnp.round(value * (LEVELS / most)).astype(jnp.int32).astype(jnp.int16)
-            move_step(i).start()
-            move_code(i).start()
-            return carry
-
-        lax.fori_loop(0, chunks, next_part, 0)
+        if h == halves - 1:
+            lax.fori_loop(0, h * chunks, send_out, 0)
+        lax.fori_loop(0, chunks, functools.partial(next_part, h, h < halves - 1), 0)
 
     for h in range(halves):
 
@@ -143,7 +147,7 @@
     rows, inner = mat_a.shape
     width = mat_b.shape[1]
     block_rows = mask_a.shape[0]
-    group = 2 if block_rows % 2 == 0 else 1
+    group = next(g for g in (4, 2, 1) if block_rows % g == 0)
     span = group * BLK
     chunks = rows // span
     halves = width // BLK
@@ -175,7 +179,7 @@
         ],
         compiler_params=pltpu.CompilerParams(collective_id=0, has_side_effects=True),
         name="cannon",
-    )(mat_a, mat_b, mask_a, mask_b)
+    )(mat_a, mat_b, mask_a.T, mask_b.T)
 
 
 def solution(mesh):

time: 80.9 us -> 61.8 us (0.76)
  Pallas kernels: 75.3 us -> 59.1 us
  local copies, waits for them, and re-layouts: 5.23 us -> 2.46 us
    pallas_call x1, Pallas kernels: 75.3 us -> 59.1 us  [body(): pl.pallas_call(functools.partial(kernel, group), out_shape=jax.ShapeDtype...]
    unnamed x3 -> x1, local copies, waits for them, and re-layouts: 5.23 us -> 2.46 us
where the time goes in v3:
time: 61.8 us; the launch traced here: 61.5 us
  Pallas kernels  59.1 us (96%)
  local copies, waits for them, and re-layouts  2.46 us (4%)
    pallas_call x1, Pallas kernels, body(): pl.pallas_call(functools.partial(kernel, group), out_shape=jax.ShapeDtype...  59.1 us
    unnamed x1, local copies, waits for them, and re-layouts  2.46 us

profile of v3, /device:TPU:0, one launch (start us, length us, event | category | flops | bytes accessed | tf_op | source)
XLA Modules:
  0.0 61.5 jit_solution(1074653279858124394)
XLA Ops:
  0.0 59.1 %cannon.1 = bf16[2560,256]{1,0:T(8,128)(2,1)} custom-call(bf16[2560,1536]{1,0:T(8,128)(2,1)} %a_hbm.1, bf16[12288,256]{1,0:T(8,128)(2,1)} %b_hbm.1, s32[12,20]{1,0:T(8,128)} %bitcast.2, s32[2,96]{1,0:T(2,128)} %bitcast.3), custom_call_target="tpu_custom_call" | custom-call | tf_op jit(solution)/shard_map/cannon/pallas_call | solution.py:156
  59.1 2.5 %copy.6 = bf16[2560,256]{1,0:T(8,128)(2,1)} copy(bf16[2560,256]{1,0:T(8,128)(2,1)} %cannon.1) | data formatting | bytes 2621440

commit v4 on v3

--- a/solution.py
+++ b/solution.py
@@ -143,6 +143,24 @@
     lax.fori_loop(0, halves * chunks, sent, 0)
 
 
+def hand_on(pieces, source, target, held, in_sem, out_sem):
+    span = source.shape[0] // pieces
+
+    def fetch(n):
+        return pltpu.make_async_copy(source.at[n * span:(n + 1) * span, :], held.at[n], in_sem.at[n])
+
+    def put(n):
+        return pltpu.make_async_copy(held.at[n], target.at[n * span:(n + 1) * span, :], out_sem.at[n])
+
+    for n in range(pieces):
+        fetch(n).start()
+    for n in range(pieces):
+        fetch(n).wait()
+        put(n).start()
+    for n in range(pieces):
+        put(n).wait()
+
+
 def body(mat_a, mat_b, mask_a, mask_b):
     rows, inner = mat_a.shape
     width = mat_b.shape[1]
@@ -153,7 +171,7 @@
     halves = width // BLK
     sends = halves * chunks
     dma = pltpu.SemaphoreType.DMA
-    return pl.pallas_call(
+    product = pl.pallas_call(
         functools.partial(kernel, group),
         out_shape=jax.ShapeDtypeStruct((rows, width), jnp.bfloat16),
         in_specs=[
@@ -180,6 +198,18 @@
         compiler_params=pltpu.CompilerParams(collective_id=0, has_side_effects=True),
         name="cannon",
     )(mat_a, mat_b, mask_a.T, mask_b.T)
+    pieces = chunks
+    return pl.pallas_call(
+        functools.partial(hand_on, pieces),
+        out_shape=jax.ShapeDtypeStruct(product.shape, product.dtype),
+        in_specs=[pl.BlockSpec(memory_space=pl.ANY)],
+        out_specs=pl.BlockSpec(memory_space=pl.ANY),
+        scratch_shapes=[
+            pltpu.VMEM((pieces, rows // pieces, width), product.dtype),
+            dma((pieces,)), dma((pieces,)),
+        ],
+        name="hand_on",
+    )(product)
 
 
 def solution(mesh):

time: 61.8 us -> 61.4 us (level)
  local copies, waits for them, and re-layouts: 2.46 us -> 0 us
  Pallas kernels: 59.1 us -> 61.2 us
    unnamed x1 -> x0, local copies, waits for them, and re-layouts: 2.46 us -> none
    pallas_call x0 -> x1, Pallas kernels: none -> 2.08 us  [body(): pl.pallas_call(functools.partial(hand_on, pieces), out_shape=jax.ShapeDty...]
where the time goes in v4:
time: 61.4 us; the launch traced here: 61.2 us
  Pallas kernels  61.2 us (100%)
    pallas_call x1, Pallas kernels, body(): pl.pallas_call(functools.partial(kernel, group), out_shape=jax.ShapeDtype...  59.1 us
    pallas_call x1, Pallas kernels, body(): pl.pallas_call(functools.partial(hand_on, pieces), out_shape=jax.ShapeDty...  2.08 us

profile of v4, /device:TPU:0, one launch (start us, length us, event | category | flops | bytes accessed | tf_op | source)
XLA Modules:
  0.0 61.2 jit_solution(4332359890618979076)
XLA Ops:
  0.0 59.1 %cannon.1.source = bf16[2560,256]{1,0:T(8,128)(2,1)} custom-call(bf16[2560,1536]{1,0:T(8,128)(2,1)} %a_hbm.1, bf16[12288,256]{1,0:T(8,128)(2,1)} %b_hbm.1, s32[12,20]{1,0:T(8,128)} %bitcast.2, s32[2,96]{1,0:T(2,128)} %bitcast.3), custom_call_target="tpu_custom_call" | custom-call | tf_op jit(solution)/shard_map/cannon/pallas_call | solution.py:174
  59.1 2.1 %hand_on.1 = bf16[2560,256]{1,0:T(8,128)(2,1)} custom-call(bf16[2560,256]{1,0:T(8,128)(2,1)} %cannon.1.source), custom_call_target="tpu_custom_call" | custom-call | tf_op jit(solution)/shard_map/hand_on/pallas_call | solution.py:202
